TPU v7x, 256 devices: a whole 4x4x8 slice. The times are simulated.
256 devices in a mesh: blk: 32 (over y_hi, z, core), rep: 8 (over x, y_lo).
Axes of the slice: x: 4, y: 4 (y_hi: 2, y_lo: 2; y = y_hi * 2 + y_lo), z: 8, core: 2. Of those that a mesh axis runs over, the one named last changes fastest.
Arguments:
- features: float32 [32768, 128], P('blk'), may hold values from -6 to 6
- factors: float32 [32768, 128], P('blk'), may hold values from -2.4 to 2.4
Outputs:
- grads: float32 [32768, 128], P(('blk', 'rep'))
All inputs are finite; a program needn't handle non-finite values.
Results may differ from a plain program's by a relative error of at most 0.00018.
Values sent between devices are 32-bit elements; how exact they have to be, the bound alone decides.
A program may use at most 128 MiB of HBM per device.

v0:
```python
import jax
import jax.numpy as jnp
from jax import lax
from jax.sharding import PartitionSpec as P


def pair_terms(own_feat, own_fac, part_feat, part_fac):
    hi = lax.Precision.HIGHEST
    width = own_feat.shape[1]
    rank = own_fac.shape[1] // 2
    cross = jnp.dot(own_feat, part_feat.T, precision=hi)
    own_sq = jnp.sum(own_feat * own_feat, axis=1)
    part_sq = jnp.sum(part_feat * part_feat, axis=1)
    kernel = jnp.exp(-(own_sq[:, None] + part_sq[None, :] - 2.0 * cross) / (2.0 * width))
    coupling = jnp.dot(own_fac[:, :rank], part_fac[:, rank:].T, precision=hi)
    coupling = coupling + jnp.dot(own_fac[:, rank:], part_fac[:, :rank].T, precision=hi)
    weight = coupling * kernel
    own_term = jnp.sum(weight, axis=1)[:, None] * own_feat - jnp.dot(
        weight, part_feat, precision=hi
    )
    return (weight, -own_term / width)


def body(features, factors):
    count = features.shape[0]
    replicas = lax.axis_size("rep")
    share = count // replicas
    first = lax.axis_index("rep") * share
    slice_feat = lax.dynamic_slice_in_dim(features, first, share, 0)
    slice_fac = lax.dynamic_slice_in_dim(factors, first, share, 0)
    weight, own_term = pair_terms(
        features,
        factors,
        lax.all_gather(slice_feat, "blk", axis=0, tiled=True),
        lax.all_gather(slice_fac, "blk", axis=0, tiled=True),
    )
    summed = lax.psum_scatter(own_term, "rep", scatter_dimension=0, tiled=True)
    return summed


def solution(mesh):
    placed = (P("blk", None), P("blk", None))
    return jax.shard_map(
        body, mesh=mesh, in_specs=placed, out_specs=P(("blk", "rep"), None), check_vma=False
    )
```

profile of v0, /device:TPU:8, one launch (start us, length us, event | category | flops | bytes accessed | tf_op | source)
XLA Modules:
  0.0 270.8 jit_solution(17942812913476998213)
XLA Ops:
  6.5 0.0 copy-start.3
  6.5 0.0 all-gather.3.cloned.1.call-start
  6.5 1.5 constant_dynamic-slice_fusion.1
  8.1 0.0 all-gather.3.cloned.1.call-update
  8.1 0.0 all-gather.5.cloned.1.call-start
  8.2 1.5 constant_dynamic-slice_fusion
  9.6 0.0 all-gather.5.cloned.1.call-update
  9.7 0.0 reduce-scatter.2.cloned.1.call-start
  9.7 1.2 multiply_reduce_fusion.1
  11.0 0.0 copy-start.2
  11.0 81.0 %all-gather.3.cloned.1.call-done = f32[4096,128]{1,0:T(8,128)} async-done(((f32[128,128]{1,0:T(8,128)}), f32[4096,128]{1,0:T(8,128)}) %all-gather.3.cloned.1.call-update) | async-done | bytes 2097168 | tf_op jit(solution)/shard_map/all_gather | solution.py:35
  92.0 0.0 copy-start.1
  92.0 17.7 %fusion.4 = f32[4096,1024]{1,0:T(8,128)} fusion(f32[4096,128]{1,0:T(8,128)} %all-gather.3.cloned.1.call-done, f32[1024,128]{1,0:T(8,128)} %param.3), kind=kOutput, calls=%fused_computation.5 | convolution fusion | flops 3221225472 | bytes 19398656 | tf_op jit(solution)/shard_map/dot_general | solution.py:16
  109.7 0.0 copy-done.3
  109.7 0.0 copy-done.1
  109.7 16.1 %fusion.6 = f32[4096,1024]{1,0:T(8,128)} fusion(f32[4096,128]{1,0:T(8,128)S(1)} %copy-done.1, f32[1024,128]{1,0:T(8,128)S(1)} %copy-done.3), kind=kOutput, calls=%fused_computation.7 | convolution fusion | flops 3221225472 | bytes 19398656 | tf_op jit(solution)/shard_map/dot_general | solution.py:15
  125.8 45.3 %all-gather.5.cloned.1.call-done = f32[4096,128]{1,0:T(8,128)} async-done(((f32[128,128]{1,0:T(8,128)}), f32[4096,128]{1,0:T(8,128)}) %all-gather.5.cloned.1.call-update) | async-done | bytes 2097168 | tf_op jit(solution)/shard_map/all_gather | solution.py:34
  171.1 2.2 multiply_reduce_fusion
  173.3 0.0 copy-done.2
  173.3 0.0 copy-start
  173.3 25.9 %fusion.12 = (f32[1024]{0:T(1024)S(1)}, f32[1024,4096]{0,1:T(8,128)}) fusion(f32[4096,128]{1,0:T(8,128)} %all-gather.5.cloned.1.call-done, f32[1024,128]{1,0:T(8,128)S(1)} %copy-done.2, f32[4096]{0:T(1024)S(1)} %multiply_reduce_fusion, f32[1024]{0:T(1024)S(1)} %multiply_reduce_fusion.1, f32[4096,1024]{1,0:T(8,128)} %fusion.6, f32[4096,1024]{1,0:T(8,128)} %fusion.4), kind=kOutput, calls=%fused_computation.18 | convolution fusion | flops 6476004352 | bytes 52977664 | tf_op jit(solution)/shard_map/dot_general | solution.py:11
  199.2 0.0 copy-done
  199.2 29.5 %fusion.9 = f32[1024,128]{1,0:T(8,128)} fusion(f32[1024,4096]{0,1:T(8,128)} %get-tuple-element.6, f32[4096,128]{1,0:T(8,128)S(1)} %copy-done, f32[1024,128]{1,0:T(8,128)S(1)} %copy-done.2, f32[1024]{0:T(1024)S(1)} %get-tuple-element.5), kind=kOutput, calls=%fused_computation.12 | convolution fusion | flops 6442975232 | bytes 19927040 | tf_op jit(solution)/shard_map/dot_general | solution.py:18
  228.7 0.0 reduce-scatter.2.cloned.1.call-update
  228.7 35.5 %reduce-scatter.2.cloned.1.call-done = f32[128,128]{1,0:T(8,128)} async-done(((f32[1024,128]{1,0:T(8,128)}), f32[128,128]{1,0:T(8,128)}) %reduce-scatter.2.cloned.1.call-update) | async-done | bytes 65552 | tf_op jit(solution)/shard_map/reduce_scatter | solution.py:37
Async XLA Ops:
  6.5 103.1 %copy-start.3 = (f32[1024,128]{1,0:T(8,128)S(1)}, f32[1024,128]{1,0:T(8,128)}, u32[]{:S(2)}) copy-start(f32[1024,128]{1,0:T(8,128)} %param.3) | copy-start | bytes 1572868
  6.5 85.4 %all-gather.3.cloned.1.call-start = ((), (), s32[]{:S(2)}) async-start(), calls=%async_computation.1 | async-start | bytes 2162688 | tf_op jit(solution)/shard_map/all_gather | solution.py:35
  8.1 163.0 %all-gather.5.cloned.1.call-start = ((), (), s32[]{:S(2)}) async-start(), calls=%async_computation.2 | async-start | bytes 2162688 | tf_op jit(solution)/shard_map/all_gather | solution.py:34
  9.7 254.6 %reduce-scatter.2.cloned.1.call-start = ((), (), s32[]{:S(2)}) async-start(), calls=%async_computation.3 | async-start | bytes 589824 | tf_op jit(solution)/shard_map/reduce_scatter | solution.py:37
  11.0 162.3 %copy-start.2 = (f32[1024,128]{1,0:T(8,128)S(1)}, f32[1024,128]{1,0:T(8,128)}, u32[]{:S(2)}) copy-start(f32[1024,128]{1,0:T(8,128)} %param.2) | copy-start | bytes 1572868
  92.0 17.7 %copy-start.1 = (f32[4096,128]{1,0:T(8,128)S(1)}, f32[4096,128]{1,0:T(8,128)}, u32[]{:S(2)}) copy-start(f32[4096,128]{1,0:T(8,128)} %all-gather.3.cloned.1.call-done) | copy-start | bytes 6291460
  173.3 25.9 %copy-start = (f32[4096,128]{1,0:T(8,128)S(1)}, f32[4096,128]{1,0:T(8,128)}, u32[]{:S(2)}) copy-start(f32[4096,128]{1,0:T(8,128)} %all-gather.5.cloned.1.call-done) | copy-start | bytes 6291460
Sparse Core Ops, SparseCore 0:
  10.1 81.8 all-gather.2
  94.8 76.3 all-gather.4
  228.9 35.3 reduce-scatter.1
where the time goes:
time: 273 us; the launch traced here: 271 us
  waiting for transfers between devices  162 us (59%)
  matrix products  89.2 us (33%)
  between operations  13.1 us (5%)
  other arithmetic  3.45 us (1%)
  local copies, waits for them, and re-layouts  3.04 us (1%)
    all_gather x1, waiting for transfers between devices, body(): lax.all_gather(slice_fac, 'blk', axis=0, tiled=True)  81 us
    all_gather x1, waiting for transfers between devices, body(): lax.all_gather(slice_feat, 'blk', axis=0, tiled=True)  45.3 us
    reduce_scatter x1, waiting for transfers between devices, body(): summed = lax.psum_scatter(own_term, 'rep', scatter_dimension=0, tiled=True)  35.5 us
    dot_general x1, matrix products, pair_terms(): jnp.dot(weight, part_feat, precision=hi)  29.5 us
    dot_general x1, matrix products, pair_terms(): cross = jnp.dot(own_feat, part_feat.T, precision=hi)  25.9 us
    dot_general x1, matrix products, pair_terms(): jnp.dot(own_fac[:, rank:], part_fac[:, :rank].T, precision=hi)  17.7 us
    dot_general x1, matrix products, pair_terms(): coupling = jnp.dot(own_fac[:, :rank], part_fac[:, rank:].T, precision=hi)  16.1 us
  transfers between devices with their start and end apart: 3, of which 3 were waited for; matrix products, arithmetic and copies ran while one was open for 13% of the time, Pallas kernels for 0%

commit v1 on v0

v1 whole, which is shorter than its diff:
```python
import functools
import math

import jax
import jax.numpy as jnp
from jax import lax
from jax.experimental import pallas as pl
from jax.experimental.pallas import tpu as pltpu
from jax.sharding import PartitionSpec as P

MESH = pl.DeviceIdType.MESH
F32, BF16 = jnp.float32, jnp.bfloat16

NAMES = ["s0", "s1", "s-1", "o0", "s2", "s-2", "o1", "s3", "s-3", "o2", "s4", "o-2", "o-1", "o3", "o-3", "o4"]
SLOT = {name: i for i, name in enumerate(NAMES)}
GROUPS = [["s0"], NAMES[1:4], NAMES[4:7], NAMES[7:10], NAMES[10:13], NAMES[13:16]]


def split(v):
    hi = v.astype(BF16)
    lo = (v - hi.astype(F32)).astype(BF16)
    return hi, lo


def kernel(count, share, width, feat, fac, out, part, x, g, y, h, f, acc, sums, stage, landed,
           recv, sent, sib_sent, local, red_sent, red_recv):
    rank = width // 2
    scale = math.log2(math.e) / (2.0 * width)
    blk, rep = lax.axis_index("blk"), lax.axis_index("rep")
    core, zpos, y_hi = blk % 2, (blk // 2) % 8, blk // 16
    y_lo = rep % 2
    down = {"blk": y_hi * 16 + (zpos + 7) % 8 * 2 + core, "rep": rep}
    up = {"blk": y_hi * 16 + (zpos + 1) % 8 * 2 + core, "rep": rep}
    side = {"blk": (1 - y_hi) * 16 + zpos * 2 + core, "rep": rep + 1 - 2 * y_lo}
    sibling = {"blk": blk + 1 - 2 * core, "rep": rep}
    pick = rep // 2 * 2 + (y_lo + y_hi) % 2
    rows = pl.ds(pl.multiple_of(pick * share, share), share)

    barrier = pltpu.get_barrier_semaphore()
    for peer in (down, up, side, sibling):
        pl.semaphore_signal(barrier, inc=1, device_id=peer, device_id_type=MESH)
    for k in range(1, 8):
        pl.semaphore_signal(barrier, inc=1, device_id={"blk": blk, "rep": (rep + k) % 8}, device_id_type=MESH)
    pl.semaphore_wait(barrier, 11)

    pending = []

    def send(name, fc, to, dst, stream=0):
        source = part.at[SLOT[name], 0, fc] if name != "s0" else (feat, fac)[fc].at[rows, :]
        sems = sent if stream == 0 else sib_sent
        copy = pltpu.make_async_remote_copy(
            src_ref=source,
            dst_ref=part.at[SLOT[dst], stream, fc],
            send_sem=sems.at[SLOT[dst], fc],
            recv_sem=recv.at[SLOT[dst], stream, fc],
            device_id=to,
            device_id_type=MESH,
        )
        copy.start()
        pending.append(copy)

    def arrive(name, fc, stream=0):
        buf = part.at[SLOT[name], stream, fc]
        sems = sent if stream == 0 else sib_sent
        pltpu.make_async_remote_copy(
            src_ref=buf, dst_ref=buf, send_sem=sems.at[SLOT[name], fc], recv_sem=recv.at[SLOT[name], stream, fc],
            device_id=sibling, device_id_type=MESH,
        ).wait_recv()

    def relay(name, fc, *onward):
        arrive(name, fc)
        for to, dst in onward:
            send(name, fc, to, dst)
        send(name, fc, sibling, name, 1)

    for fc in (0, 1):
        send("s0", fc, down, "s1")
        send("s0", fc, up, "s-1")
        send("s0", fc, side, "o0")
        send("s0", fc, sibling, "s0", 1)
    own = [
        pltpu.make_async_copy((feat, fac)[fc].at[rows, :], part.at[0, 0, fc], local.at[fc]) for fc in (0, 1)
    ]
    for copy in own:
        copy.start()

    fo = feat[...]
    norm = jnp.exp2(-scale * jnp.sum(fo * fo, axis=1, keepdims=True))
    for ref, value in ((x, fo * (2.0 * scale)), (g, fac[...] * norm)):
        hi, lo = split(value)
        for k, piece in enumerate((hi, lo, hi, lo)):
            ref[:, k * width:(k + 1) * width] = piece
    acc[...] = jnp.zeros_like(acc)
    sums[...] = jnp.zeros_like(sums)

    def prepare(names):
        for k, name in enumerate(names):
            cols = slice(k * 2 * share, (k + 1) * 2 * share)
            pf = part[SLOT[name], :, 0].reshape(2 * share, width)
            pc = part[SLOT[name], :, 1].reshape(2 * share, width)
            hi, lo = split(pf)
            f[cols, 0:width] = hi
            f[cols, width:2 * width] = lo
            hi, lo = hi.T, lo.T
            for n, piece in enumerate((hi, hi, lo, lo)):
                y[n * width:(n + 1) * width, cols] = piece
            norm = jnp.exp2(-scale * jnp.sum(pf * pf, axis=1, keepdims=True))
            hi, lo = split(pc * norm)
            hi, lo = hi.T, lo.T
            hi = jnp.concatenate([hi[rank:], hi[:rank]], axis=0)
            lo = jnp.concatenate([lo[rank:], lo[:rank]], axis=0)
            for n, piece in enumerate((hi, hi, lo, lo)):
                h[n * width:(n + 1) * width, cols] = piece

    def unit(r, points, band=256):
        mine = pl.ds(pl.multiple_of(r * band, band), band)
        s = jnp.dot(x[mine, :], y[:, :points], preferred_element_type=F32)
        c = jnp.dot(g[mine, :], h[:, :points], preferred_element_type=F32)
        w = c * jnp.exp2(s)
        total = w[:, :width]
        for k in range(1, points // width):
            total = total + w[:, k * width:(k + 1) * width]
        sums[mine, :] += total
        hi, lo = split(w)
        acc[mine, :] += jnp.dot(hi, f[:points, :], preferred_element_type=F32) + jnp.dot(
            lo, f[:points, :], preferred_element_type=F32
        )

    def bands(first, last, points):
        lax.fori_loop(first, last, lambda r, c: (unit(r, points), c)[1], 0)

    def ready(names):
        for name in names:
            for fc in (0, 1):
                arrive(name, fc, 1)
        prepare(names)

    def first_hop(fc):
        relay("s1", fc, (down, "s2"), (side, "o1"))
        relay("s-1", fc, (up, "s-2"))
        relay("o0", fc)

    def second_hop(fc):
        relay("s2", fc, (down, "s3"), (side, "o2"))
        relay("s-2", fc, (up, "s-3"))
        relay("o1", fc)

    def third_hop(fc):
        relay("s3", fc, *(((down, "s4"),) if fc == 0 else ()))
        relay("s-3", fc, *(((up, "s4"),) if fc == 1 else ()))
        relay("o2", fc, (down, "o3"))
        send("s-2", fc, side, "o-2")
        send("s-1", fc, side, "o-1")

    for copy in own:
        copy.wait()
    ready(GROUPS[0])
    bands(0, 4, 256)
    first_hop(0)
    first_hop(1)
    ready(GROUPS[1])
    bands(0, 2, 768)
    second_hop(0)
    bands(2, 4, 768)
    second_hop(1)
    ready(GROUPS[2])
    bands(0, 2, 768)
    third_hop(0)
    bands(2, 4, 768)
    third_hop(1)
    ready(GROUPS[3])
    bands(0, 2, 768)
    relay("s4", 0)
    relay("s4", 1)
    relay("o-2", 0, (up, "o-3"))
    relay("o3", 0, (down, "o4"))
    bands(2, 4, 768)
    relay("o-2", 1, (up, "o-3"))
    relay("o3", 1, (down, "o4"))
    relay("o-1", 0)
    relay("o-1", 1)
    ready(GROUPS[4])
    bands(0, 2, 768)
    relay("o-3", 0)
    relay("o4", 0)
    bands(2, 4, 768)
    relay("o-3", 1)
    relay("o4", 1)
    ready(GROUPS[5])

    def reduce_copy(k):
        return pltpu.make_async_remote_copy(
            src_ref=stage.at[k], dst_ref=landed.at[k], send_sem=red_sent.at[k], recv_sem=red_recv.at[k],
            device_id={"blk": blk, "rep": (rep // 2 + 1 + k // 2) % 4 * 2 + (y_lo + 1 + k) % 2}, device_id_type=MESH,
        )

    def finish(n, c):
        r = (rep // 2 + 1 + n) % 4
        unit(r, 768)
        for k in (0, 1):
            lane = pl.ds(pl.multiple_of((r * 2 + (y_lo + 1 + k) % 2) * share, share), share)
            row_sum = jnp.sum(sums[lane, :], axis=1, keepdims=True)
            total = row_sum * feat[lane, :] - (acc[lane, :width] + acc[lane, width:])
            stage[2 * n + k] = total * (-1.0 / width)
        return c

    for n in range(4):
        finish(n, 0)
        for k in (0, 1):
            if 2 * n + k < 7:
                reduce_copy(2 * n + k).start()
    for k in range(7):
        reduce_copy(k).wait_recv()
    total = stage[7]
    for k in range(7):
        total = total + landed[k]
    out[...] = total
    for copy in pending:
        copy.wait_send()
    for k in range(7):
        reduce_copy(k).wait_send()


def solution(mesh):
    def body(features, factors):
        count, width = features.shape
        share = count // 8
        dma = pltpu.SemaphoreType.DMA
        vmem = pltpu.VMEM
        return pl.pallas_call(
            functools.partial(kernel, count, share, width),
            out_shape=jax.ShapeDtypeStruct((share, width), F32),
            in_specs=[pl.BlockSpec(memory_space=vmem)] * 2,
            out_specs=pl.BlockSpec(memory_space=vmem),
            scratch_shapes=[
                vmem((16, 2, 2, share, width), F32),
                vmem((count, 4 * width), BF16),
                vmem((count, 4 * width), BF16),
                vmem((4 * width, 768), BF16),
                vmem((4 * width, 768), BF16),
                vmem((768, 2 * width), BF16),
                vmem((count, 2 * width), F32),
                vmem((count, width), F32),
                vmem((8, share, width), F32),
                vmem((7, share, width), F32),
                dma((16, 2, 2)),
                dma((16, 2)),
                dma((16, 2)),
                dma((2,)),
                dma((7,)),
                dma((7,)),
            ],
            compiler_params=pltpu.CompilerParams(
                collective_id=0, has_side_effects=True, vmem_limit_bytes=56 * 1024 * 1024
            ),
            name="grads",
        )(features, factors)

    placed = (P("blk", None), P("blk", None))
    return jax.shard_map(
        body, mesh=mesh, in_specs=placed, out_specs=P(("blk", "rep"), None), check_vma=False
    )
```

time: 273 us -> 54.3 us (0.20)
  waiting for transfers between devices: 162 us -> 0 us
  matrix products: 89.2 us -> 0 us
  Pallas kernels: 0 us -> 52 us
  between operations: 13.1 us -> 0.01 us
  other arithmetic: 3.45 us -> 0 us
    all_gather x2 -> x0, waiting for transfers between devices: 126 us -> none  [the longest x1 81 us: body(): lax.all_gather(slice_fac, 'blk', axis=0, tiled=True)]
    dot_general x4 -> x0, matrix products: 89.2 us -> none  [the longest x1 29.5 us: pair_terms(): jnp.dot(weight, part_feat, precision=hi)]
    pallas_call x0 -> x1, Pallas kernels: none -> 52 us  [body(): pl.pallas_call(functools.partial(kernel, count, share, width), out_shape=...]
    reduce_scatter x1 -> x0, waiting for transfers between devices: 35.5 us -> none  [body(): summed = lax.psum_scatter(own_term, 'rep', scatter_dimension=0, tiled=True)]
    reduce_sum x2 -> x0, other arithmetic: 3.45 us -> none  [the longest x1 2.2 us: pair_terms(): part_sq = jnp.sum(part_feat * part_feat, axis=1)]
    dynamic_slice x2 -> x0, local copies, waits for them, and re-layouts: 3.02 us -> none  [the longest x1 1.54 us: body(): slice_fac = lax.dynamic_slice_in_dim(factors, first, share, 0)]
  transfers between devices with their start and end apart: 3 -> 0, of which waited for: 3 -> 0; matrix products, arithmetic and copies ran while one was open for 13% -> 0% of each run, Pallas kernels for 0% -> 0%
where the time goes in v1:
time: 54.3 us; the launch traced here: 53.4 us
  Pallas kernels  52 us (96%)
  local copies, waits for them, and re-layouts  1.47 us (3%)
    pallas_call x1, Pallas kernels, body(): pl.pallas_call(functools.partial(kernel, count, share, width), out_shape=...  52 us
    unnamed x1, local copies, waits for them, and re-layouts  1.47 us

profile of v1, /device:TPU:8, one launch (start us, length us, event | category | flops | bytes accessed | tf_op | source)
XLA Modules:
  0.0 53.4 jit_solution(11185324933498417357)
XLA Ops:
  0.0 52.0 %grads.1 = f32[128,128]{1,0:T(8,128)} custom-call(f32[1024,128]{1,0:T(8,128)} %feat.1, f32[1024,128]{1,0:T(8,128)} %fac.1), custom_call_target="tpu_custom_call" | custom-call | tf_op jit(solution)/shard_map/grads/pallas_call | solution.py:230
  52.0 1.5 %copy.4 = f32[128,128]{1,0:T(8,128)} copy(f32[128,128]{1,0:T(8,128)} %grads.1) | data formatting | bytes 131072

commit v2 on v1

v2 whole, which is shorter than its diff:
```python
import functools
import math

import jax
import jax.numpy as jnp
from jax import lax
from jax.experimental import pallas as pl
from jax.experimental.pallas import tpu as pltpu
from jax.sharding import PartitionSpec as P

MESH = pl.DeviceIdType.MESH
F32, BF16 = jnp.float32, jnp.bfloat16

NAMES = ["s0", "s1", "s-1", "o0", "s2", "s-2", "o1", "s3", "s-3", "o2", "o3", "s4", "o-2", "o4", "o-3", "o-1"]
SLOT = {name: i for i, name in enumerate(NAMES)}
SOURCES = [("s0", "s0", "s0"), ("s1", "s-1", "s1"), ("s2", "s-2", "s2"), ("o2", "s-3", "s-2"), ("o3", "o-2", "s-1")]


def split(v):
    hi = v.astype(BF16)
    lo = (v - hi.astype(F32)).astype(BF16)
    return hi, lo


def kernel(count, share, width, feat, fac, out, part, x, g, y, h, f, acc, sums, stage, landed,
           recv, sib_recv, sent, sib_sent, local, red_sent, red_recv):
    rank = width // 2
    scale = math.log2(math.e) / (2.0 * width)
    blk, rep = lax.axis_index("blk"), lax.axis_index("rep")
    core, zpos, y_hi = blk % 2, (blk // 2) % 8, blk // 16
    y_lo = rep % 2
    down = {"blk": y_hi * 16 + (zpos + 7) % 8 * 2 + core, "rep": rep}
    up = {"blk": y_hi * 16 + (zpos + 1) % 8 * 2 + core, "rep": rep}
    side = {"blk": (1 - y_hi) * 16 + zpos * 2 + core, "rep": rep + 1 - 2 * y_lo}
    sibling = {"blk": blk + 1 - 2 * core, "rep": rep}
    pick = rep // 2 * 2 + (y_lo + y_hi) % 2
    rows = pl.ds(pl.multiple_of(pick * share, share), share)

    barrier = pltpu.get_barrier_semaphore()
    for peer in (down, up, side, sibling):
        pl.semaphore_signal(barrier, inc=1, device_id=peer, device_id_type=MESH)
    for k in range(1, 8):
        pl.semaphore_signal(barrier, inc=1, device_id={"blk": blk, "rep": (rep + k) % 8}, device_id_type=MESH)
    pl.semaphore_wait(barrier, 11)

    def remote(src, dst, send_sem, recv_sem, to):
        return pltpu.make_async_remote_copy(
            src_ref=src, dst_ref=dst, send_sem=send_sem, recv_sem=recv_sem, device_id=to, device_id_type=MESH
        )

    def send_round(k, fc):
        for n, (name, to) in enumerate(zip(SOURCES[k - 1], (down, up, side))):
            source = part.at[0, fc, SLOT[name]] if name != "s0" else (feat, fac)[fc].at[rows, :]
            remote(source, part.at[0, fc, 3 * k - 2 + n], sent, recv.at[k, fc], to).start()

    def of_round(stream, k, fc):
        return part.at[stream, fc, pl.ds(3 * k - 2, 3)]

    def take_round(k, fc):
        mine, theirs = of_round(0, k, fc), of_round(1, k, fc)
        remote(mine, mine, sent, recv.at[k, fc], sibling).wait_recv()
        if k < 5:
            send_round(k + 1, fc)
        remote(mine, theirs, sib_sent, sib_recv.at[k, fc], sibling).start()

    def take_sibling(k):
        for fc in (0, 1):
            buf = of_round(1, k, fc) if k else part.at[1, fc, 0]
            remote(buf, buf, sib_sent, sib_recv.at[k, fc], sibling).wait_recv()

    for fc in (0, 1):
        send_round(1, fc)
    for fc in (0, 1):
        remote((feat, fac)[fc].at[rows, :], part.at[1, fc, 0], sib_sent, sib_recv.at[0, fc], sibling).start()
    own = [
        pltpu.make_async_copy((feat, fac)[fc].at[rows, :], part.at[0, fc, 0], local.at[fc]) for fc in (0, 1)
    ]
    for copy in own:
        copy.start()

    fo = feat[...]
    norm = jnp.exp2(-scale * jnp.sum(fo * fo, axis=1, keepdims=True))
    for ref, value in ((x, fo * (2.0 * scale)), (g, fac[...] * norm)):
        hi, lo = split(value)
        for k, piece in enumerate((hi, lo, hi, lo)):
            ref[:, k * width:(k + 1) * width] = piece
    acc[...] = jnp.zeros_like(acc)
    sums[...] = jnp.zeros_like(sums)

    def prepare(col, stream, slot, slots):
        points = slots * share
        cols = slice(col, col + points)
        pf = part[stream, 0, slot:slot + slots].reshape(points, width)
        pc = part[stream, 1, slot:slot + slots].reshape(points, width)
        hi, lo = split(pf)
        f[cols, 0:width] = hi
        f[cols, width:2 * width] = lo
        hi, lo = hi.T, lo.T
        for n, piece in enumerate((hi, hi, lo, lo)):
            y[n * width:(n + 1) * width, cols] = piece
        norm = jnp.exp2(-scale * jnp.sum(pf * pf, axis=1, keepdims=True))
        hi, lo = split(pc * norm)
        hi, lo = hi.T, lo.T
        hi = jnp.concatenate([hi[rank:], hi[:rank]], axis=0)
        lo = jnp.concatenate([lo[rank:], lo[:rank]], axis=0)
        for n, piece in enumerate((hi, hi, lo, lo)):
            h[n * width:(n + 1) * width, cols] = piece

    def unit(r, points, band=256):
        mine = pl.ds(r * band, band) if isinstance(r, int) else pl.ds(pl.multiple_of(r * band, band), band)
        s = jnp.dot(x[mine, :], y[:, :points], preferred_element_type=F32)
        c = jnp.dot(g[mine, :], h[:, :points], preferred_element_type=F32)
        w = c * jnp.exp2(s)
        total = w[:, :width]
        for k in range(1, points // width):
            total = total + w[:, k * width:(k + 1) * width]
        sums[mine, :] += total
        hi, lo = split(w)
        acc[mine, :] += jnp.dot(hi, f[:points, :], preferred_element_type=F32) + jnp.dot(
            lo, f[:points, :], preferred_element_type=F32
        )

    def bands(first, last, points):
        for r in range(first, last):
            unit(r, points)

    third = 3 * share
    for copy in own:
        copy.wait()
    take_sibling(0)
    prepare(0, 0, 0, 1)
    prepare(share, 1, 0, 1)
    bands(0, 4, 2 * share)
    take_round(1, 0)
    take_round(1, 1)
    for k in (1, 2, 3, 4):
        points = third if k == 1 else 2 * third
        prepare(0, 0, 3 * k - 2, 3)
        if k > 1:
            take_sibling(k - 1)
            prepare(third, 1, 3 * k - 5, 3)
        bands(0, 3, points)
        take_round(k + 1, 0)
        bands(3, 4, points)
        take_round(k + 1, 1)
    take_sibling(4)
    prepare(0, 1, 10, 3)
    bands(0, 4, third)
    take_sibling(5)
    prepare(0, 0, 13, 3)
    prepare(third, 1, 13, 3)

    def reduce_copy(k):
        to = {"blk": blk, "rep": (rep // 2 + 1 + k // 2) % 4 * 2 + (y_lo + 1 + k) % 2}
        return remote(stage.at[k], landed.at[k], red_sent, red_recv, to)

    def finish(n, c):
        r = (rep // 2 + 1 + n) % 4
        unit(r, 768)
        for k in (0, 1):
            lane = pl.ds(pl.multiple_of((r * 2 + (y_lo + 1 + k) % 2) * share, share), share)
            row_sum = jnp.sum(sums[lane, :], axis=1, keepdims=True)
            total = row_sum * feat[lane, :] - (acc[lane, :width] + acc[lane, width:])
            stage[2 * n + k] = total * (-1.0 / width)
        return c

    for n in range(4):
        finish(n, 0)
        for k in (0, 1):
            if 2 * n + k < 7:
                reduce_copy(2 * n + k).start()
    reduced = remote(stage.at[pl.ds(0, 7)], landed, red_sent, red_recv, sibling)
    reduced.wait_recv()
    total = stage[7]
    for k in range(7):
        total = total + landed[k]
    out[...] = total
    reduced.wait_send()
    for fc in (0, 1):
        gathered = part.at[0, fc, pl.ds(1, 15)]
        remote(gathered, gathered, sent, recv.at[0, 0], sibling).wait_send()
    remote(part.at[1], part.at[1], sib_sent, recv.at[0, 0], sibling).wait_send()


def solution(mesh):
    def body(features, factors):
        count, width = features.shape
        share = count // 8
        dma = pltpu.SemaphoreType.DMA
        vmem = pltpu.VMEM
        return pl.pallas_call(
            functools.partial(kernel, count, share, width),
            out_shape=jax.ShapeDtypeStruct((share, width), F32),
            in_specs=[pl.BlockSpec(memory_space=vmem)] * 2,
            out_specs=pl.BlockSpec(memory_space=vmem),
            scratch_shapes=[
                vmem((2, 2, 16, share, width), F32),
                vmem((count, 4 * width), BF16),
                vmem((count, 4 * width), BF16),
                vmem((4 * width, 768), BF16),
                vmem((4 * width, 768), BF16),
                vmem((768, 2 * width), BF16),
                vmem((count, 2 * width), F32),
                vmem((count, width), F32),
                vmem((8, share, width), F32),
                vmem((7, share, width), F32),
                dma((6, 2)),
                dma((6, 2)),
                dma,
                dma,
                dma((2,)),
                dma,
                dma,
            ],
            compiler_params=pltpu.CompilerParams(
                collective_id=0, has_side_effects=True, vmem_limit_bytes=56 * 1024 * 1024
            ),
            name="grads",
        )(features, factors)

    placed = (P("blk", None), P("blk", None))
    return jax.shard_map(
        body, mesh=mesh, in_specs=placed, out_specs=P(("blk", "rep"), None), check_vma=False
    )
```

time: 54.3 us -> 45.4 us (0.84); the launches traced: 53.4 us -> 45.3 us
  Pallas kernels: 52 us -> 43.8 us
    pallas_call x1, Pallas kernels: 52 us -> 43.8 us  [body(): pl.pallas_call(functools.partial(kernel, count, share, width), out_shape=...]
where the time goes in v2:
time: 45.4 us; the launch traced here: 45.3 us
  Pallas kernels  43.8 us (96%)
  local copies, waits for them, and re-layouts  1.47 us (3%)
    pallas_call x1, Pallas kernels, body(): pl.pallas_call(functools.partial(kernel, count, share, width), out_shape=...  43.8 us
    unnamed x1, local copies, waits for them, and re-layouts  1.47 us

profile of v2, /device:TPU:8, one launch (start us, length us, event | category | flops | bytes accessed | tf_op | source)
XLA Modules:
  0.0 45.3 jit_solution(13206155048308956449)
XLA Ops:
  0.0 43.8 %grads.1 = f32[128,128]{1,0:T(8,128)} custom-call(f32[1024,128]{1,0:T(8,128)} %feat.1, f32[1024,128]{1,0:T(8,128)} %fac.1), custom_call_target="tpu_custom_call" | custom-call | tf_op jit(solution)/shard_map/grads/pallas_call | solution.py:191
  43.8 1.5 %copy.4 = f32[128,128]{1,0:T(8,128)} copy(f32[128,128]{1,0:T(8,128)} %grads.1) | data formatting | bytes 131072

commit v3 on v2

--- a/solution.py
+++ b/solution.py
@@ -16,14 +16,17 @@
 SOURCES = [("s0", "s0", "s0"), ("s1", "s-1", "s1"), ("s2", "s-2", "s2"), ("o2", "s-3", "s-2"), ("o3", "o-2", "s-1")]
 
 
+STEPS = (2, 1, 3, 0)
+
+
 def split(v):
     hi = v.astype(BF16)
     lo = (v - hi.astype(F32)).astype(BF16)
     return hi, lo
 
 
-def kernel(count, share, width, feat, fac, out, part, x, g, y, h, f, acc, sums, stage, landed,
-           recv, sib_recv, sent, sib_sent, local, red_sent, red_recv):
+def kernel(count, share, width, feat_in, fac_in, out, feat, fac, part, x, g, y, h, f, acc, sums, stage, landed,
+           recv, side_recv, sib_recv, sent, sib_sent, local, loaded, red_sent, red_recv):
     rank = width // 2
     scale = math.log2(math.e) / (2.0 * width)
     blk, rep = lax.axis_index("blk"), lax.axis_index("rep")
@@ -41,6 +44,11 @@
         pl.semaphore_signal(barrier, inc=1, device_id=peer, device_id_type=MESH)
     for k in range(1, 8):
         pl.semaphore_signal(barrier, inc=1, device_id={"blk": blk, "rep": (rep + k) % 8}, device_id_type=MESH)
+    loads = [
+        pltpu.make_async_copy((feat_in, fac_in)[fc], (feat, fac)[fc], loaded.at[fc]) for fc in (0, 1)
+    ]
+    for copy in loads:
+        copy.start()
     pl.semaphore_wait(barrier, 11)
 
     def remote(src, dst, send_sem, recv_sem, to):
@@ -48,20 +56,27 @@
             src_ref=src, dst_ref=dst, send_sem=send_sem, recv_sem=recv_sem, device_id=to, device_id_type=MESH
         )
 
-    def send_round(k, fc):
+    def send_round(k, fc, names):
         for n, (name, to) in enumerate(zip(SOURCES[k - 1], (down, up, side))):
-            source = part.at[0, fc, SLOT[name]] if name != "s0" else (feat, fac)[fc].at[rows, :]
-            remote(source, part.at[0, fc, 3 * k - 2 + n], sent, recv.at[k, fc], to).start()
+            if name in names:
+                source = part.at[0, fc, SLOT[name]] if name != "s0" else (feat_in, fac_in)[fc].at[rows, :]
+                sem = (side_recv if n == 2 else recv).at[k, fc]
+                remote(source, part.at[0, fc, 3 * k - 2 + n], sent, sem, to).start()
 
     def of_round(stream, k, fc):
         return part.at[stream, fc, pl.ds(3 * k - 2, 3)]
 
     def take_round(k, fc):
-        mine, theirs = of_round(0, k, fc), of_round(1, k, fc)
-        remote(mine, mine, sent, recv.at[k, fc], sibling).wait_recv()
+        last = NAMES[3 * k]
+        along = part.at[0, fc, pl.ds(3 * k - 2, 2)]
+        remote(along, along, sent, recv.at[k, fc], sibling).wait_recv()
         if k < 5:
-            send_round(k + 1, fc)
-        remote(mine, theirs, sib_sent, sib_recv.at[k, fc], sibling).start()
+            send_round(k + 1, fc, [name for name in NAMES if name != last])
+        across = part.at[0, fc, 3 * k]
+        remote(across, across, sent, side_recv.at[k, fc], sibling).wait_recv()
+        if k < 5:
+            send_round(k + 1, fc, [last])
+        remote(of_round(0, k, fc), of_round(1, k, fc), sib_sent, sib_recv.at[k, fc], sibling).start()
 
     def take_sibling(k):
         for fc in (0, 1):
@@ -69,15 +84,17 @@
             remote(buf, buf, sib_sent, sib_recv.at[k, fc], sibling).wait_recv()
 
     for fc in (0, 1):
-        send_round(1, fc)
+        send_round(1, fc, ["s0"])
     for fc in (0, 1):
-        remote((feat, fac)[fc].at[rows, :], part.at[1, fc, 0], sib_sent, sib_recv.at[0, fc], sibling).start()
+        remote((feat_in, fac_in)[fc].at[rows, :], part.at[1, fc, 0], sib_sent, sib_recv.at[0, fc], sibling).start()
     own = [
-        pltpu.make_async_copy((feat, fac)[fc].at[rows, :], part.at[0, fc, 0], local.at[fc]) for fc in (0, 1)
+        pltpu.make_async_copy((feat_in, fac_in)[fc].at[rows, :], part.at[0, fc, 0], local.at[fc]) for fc in (0, 1)
     ]
     for copy in own:
         copy.start()
 
+    for copy in loads:
+        copy.wait()
     fo = feat[...]
     norm = jnp.exp2(-scale * jnp.sum(fo * fo, axis=1, keepdims=True))
     for ref, value in ((x, fo * (2.0 * scale)), (g, fac[...] * norm)):
@@ -130,13 +147,15 @@
     take_sibling(0)
     prepare(0, 0, 0, 1)
     prepare(share, 1, 0, 1)
-    bands(0, 4, 2 * share)
     take_round(1, 0)
     take_round(1, 1)
     for k in (1, 2, 3, 4):
-        points = third if k == 1 else 2 * third
-        prepare(0, 0, 3 * k - 2, 3)
-        if k > 1:
+        if k == 1:
+            points = 2 * share + third
+            prepare(2 * share, 0, 1, 3)
+        else:
+            points = 2 * third
+            prepare(0, 0, 3 * k - 2, 3)
             take_sibling(k - 1)
             prepare(third, 1, 3 * k - 5, 3)
         bands(0, 3, points)
@@ -145,30 +164,33 @@
         take_round(k + 1, 1)
     take_sibling(4)
     prepare(0, 1, 10, 3)
-    bands(0, 4, third)
+    prepare(third, 0, 13, 3)
+    bands(0, 4, 2 * third)
     take_sibling(5)
-    prepare(0, 0, 13, 3)
-    prepare(third, 1, 13, 3)
+    prepare(0, 1, 13, 3)
 
     def reduce_copy(k):
-        to = {"blk": blk, "rep": (rep // 2 + 1 + k // 2) % 4 * 2 + (y_lo + 1 + k) % 2}
+        to = {"blk": blk, "rep": (rep // 2 + STEPS[k // 2]) % 4 * 2 + (y_lo + 1 + k) % 2}
         return remote(stage.at[k], landed.at[k], red_sent, red_recv, to)
 
-    def finish(n, c):
-        r = (rep // 2 + 1 + n) % 4
-        unit(r, 768)
-        for k in (0, 1):
-            lane = pl.ds(pl.multiple_of((r * 2 + (y_lo + 1 + k) % 2) * share, share), share)
-            row_sum = jnp.sum(sums[lane, :], axis=1, keepdims=True)
-            total = row_sum * feat[lane, :] - (acc[lane, :width] + acc[lane, width:])
-            stage[2 * n + k] = total * (-1.0 / width)
-        return c
-
-    for n in range(4):
-        finish(n, 0)
-        for k in (0, 1):
-            if 2 * n + k < 7:
-                reduce_copy(2 * n + k).start()
+    def finish(k):
+        r = (rep // 2 + STEPS[k // 2]) % 4 * 2 + (y_lo + 1 + k) % 2
+        lane = pl.ds(pl.multiple_of(r * share, share), share)
+        row_sum = jnp.sum(sums[lane, :], axis=1, keepdims=True)
+        total = row_sum * feat[lane, :] - (acc[lane, :width] + acc[lane, width:])
+        stage[k] = total * (-1.0 / width)
+
+    for n in range(3):
+        unit((rep // 2 + STEPS[n]) % 4, third)
+        finish(2 * n)
+        finish(2 * n + 1)
+        reduce_copy(2 * n).start()
+        reduce_copy(2 * n + 1).start()
+    unit(rep + 1 - 2 * y_lo, third, share)
+    finish(6)
+    reduce_copy(6).start()
+    unit(rep, third, share)
+    finish(7)
     reduced = remote(stage.at[pl.ds(0, 7)], landed, red_sent, red_recv, sibling)
     reduced.wait_recv()
     total = stage[7]
@@ -191,9 +213,11 @@
         return pl.pallas_call(
             functools.partial(kernel, count, share, width),
             out_shape=jax.ShapeDtypeStruct((share, width), F32),
-            in_specs=[pl.BlockSpec(memory_space=vmem)] * 2,
+            in_specs=[pl.BlockSpec(memory_space=pl.ANY)] * 2,
             out_specs=pl.BlockSpec(memory_space=vmem),
             scratch_shapes=[
+                vmem((count, width), F32),
+                vmem((count, width), F32),
                 vmem((2, 2, 16, share, width), F32),
                 vmem((count, 4 * width), BF16),
                 vmem((count, 4 * width), BF16),
@@ -206,14 +230,16 @@
                 vmem((7, share, width), F32),
                 dma((6, 2)),
                 dma((6, 2)),
-                dma,
-                dma,
+                dma((6, 2)),
+                dma,
+                dma,
+                dma((2,)),
                 dma((2,)),
                 dma,
                 dma,
             ],
             compiler_params=pltpu.CompilerParams(
-                collective_id=0, has_side_effects=True, vmem_limit_bytes=56 * 1024 * 1024
+                collective_id=0, has_side_effects=True
             ),
             name="grads",
         )(features, factors)

time: 45.4 us -> 44.7 us (0.985); the launches traced: 45.3 us -> 44.1 us
  Pallas kernels: 43.8 us -> 42.7 us
    pallas_call x1, Pallas kernels: 43.8 us -> 42.7 us  [body(): pl.pallas_call(functools.partial(kernel, count, share, width), out_shape=...]
where the time goes in v3:
time: 44.7 us; the launch traced here: 44.1 us
  Pallas kernels  42.7 us (96%)
  local copies, waits for them, and re-layouts  1.47 us (3%)
    pallas_call x1, Pallas kernels, body(): pl.pallas_call(functools.partial(kernel, count, share, width), out_shape=...  42.7 us
    unnamed x1, local copies, waits for them, and re-layouts  1.47 us

profile of v3, /device:TPU:8, one launch (start us, length us, event | category | flops | bytes accessed | tf_op | source)
XLA Modules:
  0.0 44.1 jit_solution(10391596997793278414)
XLA Ops:
  0.0 42.7 %grads.1 = f32[128,128]{1,0:T(8,128)} custom-call(f32[1024,128]{1,0:T(8,128)} %feat_in.1, f32[1024,128]{1,0:T(8,128)} %fac_in.1), custom_call_target="tpu_custom_call" | custom-call | tf_op jit(solution)/shard_map/grads/pallas_call | solution.py:213
  42.7 1.5 %copy.4 = f32[128,128]{1,0:T(8,128)} copy(f32[128,128]{1,0:T(8,128)} %grads.1) | data formatting | bytes 131072

commit v4 on v3

--- a/solution.py
+++ b/solution.py
@@ -56,26 +56,35 @@
             src_ref=src, dst_ref=dst, send_sem=send_sem, recv_sem=recv_sem, device_id=to, device_id_type=MESH
         )
 
-    def send_round(k, fc, names):
+    half = share // 2
+
+    def send_round(k, fc, cut, names):
         for n, (name, to) in enumerate(zip(SOURCES[k - 1], (down, up, side))):
             if name in names:
-                source = part.at[0, fc, SLOT[name]] if name != "s0" else (feat_in, fac_in)[fc].at[rows, :]
-                sem = (side_recv if n == 2 else recv).at[k, fc]
-                remote(source, part.at[0, fc, 3 * k - 2 + n], sent, sem, to).start()
+                points = pl.ds(cut * half, half)
+                if name == "s0":
+                    first = pl.multiple_of(pick * share + cut * half, half)
+                    source = (feat_in, fac_in)[fc].at[pl.ds(first, half), :]
+                else:
+                    source = part.at[0, fc, SLOT[name], points]
+                sem = (side_recv if n == 2 else recv).at[k, fc, cut]
+                remote(source, part.at[0, fc, 3 * k - 2 + n, points], sent, sem, to).start()
 
     def of_round(stream, k, fc):
         return part.at[stream, fc, pl.ds(3 * k - 2, 3)]
 
     def take_round(k, fc):
         last = NAMES[3 * k]
-        along = part.at[0, fc, pl.ds(3 * k - 2, 2)]
-        remote(along, along, sent, recv.at[k, fc], sibling).wait_recv()
-        if k < 5:
-            send_round(k + 1, fc, [name for name in NAMES if name != last])
-        across = part.at[0, fc, 3 * k]
-        remote(across, across, sent, side_recv.at[k, fc], sibling).wait_recv()
-        if k < 5:
-            send_round(k + 1, fc, [last])
+        for cut in (0, 1):
+            points = pl.ds(cut * half, half)
+            along = part.at[0, fc, pl.ds(3 * k - 2, 2), points]
+            remote(along, along, sent, recv.at[k, fc, cut], sibling).wait_recv()
+            if k < 5:
+                send_round(k + 1, fc, cut, [name for name in NAMES if name != last])
+            across = part.at[0, fc, 3 * k, points]
+            remote(across, across, sent, side_recv.at[k, fc, cut], sibling).wait_recv()
+            if k < 5:
+                send_round(k + 1, fc, cut, [last])
         remote(of_round(0, k, fc), of_round(1, k, fc), sib_sent, sib_recv.at[k, fc], sibling).start()
 
     def take_sibling(k):
@@ -84,7 +93,8 @@
             remote(buf, buf, sib_sent, sib_recv.at[k, fc], sibling).wait_recv()
 
     for fc in (0, 1):
-        send_round(1, fc, ["s0"])
+        for cut in (0, 1):
+            send_round(1, fc, cut, ["s0"])
     for fc in (0, 1):
         remote((feat_in, fac_in)[fc].at[rows, :], part.at[1, fc, 0], sib_sent, sib_recv.at[0, fc], sibling).start()
     own = [
@@ -200,8 +210,8 @@
     reduced.wait_send()
     for fc in (0, 1):
         gathered = part.at[0, fc, pl.ds(1, 15)]
-        remote(gathered, gathered, sent, recv.at[0, 0], sibling).wait_send()
-    remote(part.at[1], part.at[1], sib_sent, recv.at[0, 0], sibling).wait_send()
+        remote(gathered, gathered, sent, recv.at[0, 0, 0], sibling).wait_send()
+    remote(part.at[1], part.at[1], sib_sent, recv.at[0, 0, 0], sibling).wait_send()
 
 
 def solution(mesh):
@@ -228,8 +238,8 @@
                 vmem((count, width), F32),
                 vmem((8, share, width), F32),
                 vmem((7, share, width), F32),
-                dma((6, 2)),
-                dma((6, 2)),
+                dma((6, 2, 2)),
+                dma((6, 2, 2)),
                 dma((6, 2)),
                 dma,
                 dma,

time: 44.7 us -> 43.8 us (0.980)
  Pallas kernels: 42.7 us -> 42.1 us
    pallas_call x1, Pallas kernels: 42.7 us -> 42.1 us  [body(): pl.pallas_call(functools.partial(kernel, count, share, width), out_shape=...]
where the time goes in v4:
time: 43.8 us; the launch traced here: 43.6 us
  Pallas kernels  42.1 us (96%)
  local copies, waits for them, and re-layouts  1.47 us (3%)
    pallas_call x1, Pallas kernels, body(): pl.pallas_call(functools.partial(kernel, count, share, width), out_shape=...  42.1 us
    unnamed x1, local copies, waits for them, and re-layouts  1.47 us

profile of v4, /device:TPU:8, one launch (start us, length us, event | category | flops | bytes accessed | tf_op | source)
XLA Modules:
  0.0 43.6 jit_solution(9270101692695271524)
XLA Ops:
  0.0 42.1 %grads.1 = f32[128,128]{1,0:T(8,128)} custom-call(f32[1024,128]{1,0:T(8,128)} %feat_in.1, f32[1024,128]{1,0:T(8,128)} %fac_in.1), custom_call_target="tpu_custom_call" | custom-call | tf_op jit(solution)/shard_map/grads/pallas_call | solution.py:223
  42.1 1.5 %copy.4 = f32[128,128]{1,0:T(8,128)} copy(f32[128,128]{1,0:T(8,128)} %grads.1) | data formatting | bytes 131072

commit v5 on v4

--- a/solution.py
+++ b/solution.py
@@ -81,7 +81,8 @@
             remote(along, along, sent, recv.at[k, fc, cut], sibling).wait_recv()
             if k < 5:
                 send_round(k + 1, fc, cut, [name for name in NAMES if name != last])
-            across = part.at[0, fc, 3 * k, points]
+        for cut in (0, 1):
+            across = part.at[0, fc, 3 * k, pl.ds(cut * half, half)]
             remote(across, across, sent, side_recv.at[k, fc, cut], sibling).wait_recv()
             if k < 5:
                 send_round(k + 1, fc, cut, [last])

time: 43.8 us -> 44.3 us (1.011)
  no operation moved by 1% of the time
where the time goes in v5:
time: 44.3 us; the launch traced here: 43.7 us
  Pallas kernels  42.2 us (95%)
  local copies, waits for them, and re-layouts  1.47 us (3%)
    pallas_call x1, Pallas kernels, body(): pl.pallas_call(functools.partial(kernel, count, share, width), out_shape=...  42.2 us
    unnamed x1, local copies, waits for them, and re-layouts  1.47 us

profile of v5, /device:TPU:8, one launch (start us, length us, event | category | flops | bytes accessed | tf_op | source)
XLA Modules:
  0.0 43.7 jit_solution(15737509170919612597)
XLA Ops:
  0.0 42.2 %grads.1 = f32[128,128]{1,0:T(8,128)} custom-call(f32[1024,128]{1,0:T(8,128)} %feat_in.1, f32[1024,128]{1,0:T(8,128)} %fac_in.1), custom_call_target="tpu_custom_call" | custom-call | tf_op jit(solution)/shard_map/grads/pallas_call | solution.py:224
  42.2 1.5 %copy.4 = f32[128,128]{1,0:T(8,128)} copy(f32[128,128]{1,0:T(8,128)} %grads.1) | data formatting | bytes 131072
